TPU v7x, 32 devices: a whole 2x2x4 slice. The times are simulated.
32 devices in a mesh: dom: 2 (over y), blk: 4 (over z), sub: 2 (over x), rep: 2 (over core).
Axes of the slice: x: 2, y: 2, z: 4, core: 2. Of those that a mesh axis runs over, the one named last changes fastest.
Arguments:
- tokens: bfloat16 [4096, 2048], P(('dom', 'blk', 'sub', 'rep')), parts along dimension 0, may hold values from -6 to 6
- expert_ids: int32 [4096, 8], P(('dom', 'blk', 'sub', 'rep')), parts along dimension 0, may hold values from 0 to 127, as said below
- gate_weights: float32 [4096, 8], P(('dom', 'blk', 'sub', 'rep')), parts along dimension 0, may hold values from 0.2 to 2
- w_gate: bfloat16 [2, 768, 2048], P('sub', 'rep', 'blk'), may hold values from -0.125 to 0.125
- w_up: bfloat16 [2, 768, 2048], P('sub', 'rep', 'blk'), may hold values from -0.125 to 0.125
- w_down: bfloat16 [2, 768, 2048], P('sub', 'rep', 'blk'), may hold values from -0.21875 to 0.21875
- cotangent: bfloat16 [4096, 2048], P(('dom', 'blk', 'sub', 'rep')), parts along dimension 0, may hold values from -6 to 6
Outputs:
- mixed: bfloat16 [4096, 2048], P(('dom', 'blk', 'sub', 'rep')), parts along dimension 0
- token_grad: bfloat16 [4096, 2048], P(('dom', 'blk', 'sub', 'rep')), parts along dimension 0
- gate_grad: float32 [4096, 8], P(('dom', 'blk', 'sub', 'rep')), parts along dimension 0
- grad_gate: float32 [4, 768, 2048], P(('dom', 'sub'), 'rep', 'blk'), parts along dimension 0
- grad_up: float32 [4, 768, 2048], P(('dom', 'sub'), 'rep', 'blk'), parts along dimension 0
- grad_down: float32 [4, 768, 2048], P(('dom', 'sub'), 'rep', 'blk'), parts along dimension 0
There are 2 independent parts, one for each index of `dom`. A program takes and returns all parts, laid end to end along the dimension named above; an argument that names none is the same for every part. Nothing has to cross between parts.
Inputs may be any that keep to these rules, and one draw needn't show every extreme that they name: `expert_ids`: each row names 8 different experts. Among the 128 rows of one device, each expert below 2 is named by 1 to 12 rows, and in every draw some expert below 2 is named by 12 rows on every device of one blk index.
All inputs are finite; a program needn't handle non-finite values.
Results may differ from a plain program's by a relative error of at most 0.02.
Values may be sent and summed in bfloat16 or wider, within the bound.
No kernel may reach another device: no remote copies, remote signals or barrier semaphores. Data moves between devices by JAX's collectives and lax.ppermute only.
A program may use at most 64 MiB of HBM per device.

v0:
```python
import jax
import jax.numpy as jnp
from jax import lax
from jax.sharding import PartitionSpec as P

NUM_EXPERTS = 128
TOPK = 8
CAP = 12


def silu_pair(pre_act):
    sigmoid_v = jax.nn.sigmoid(pre_act)
    return (pre_act * sigmoid_v, sigmoid_v * (1.0 + pre_act * (1.0 - sigmoid_v)))


def on_device(tokens, expert_ids, gate_weights, w_gate, w_up, w_down, cotangent):
    tok_count = tokens.shape[0]
    local_experts = w_gate.shape[0]
    n_window = local_experts * lax.axis_size("sub")
    capacity = CAP
    total_tokens = tok_count * lax.axis_size("blk") * lax.axis_size("sub") * lax.axis_size("rep")
    grad_scale = (total_tokens * TOPK / NUM_EXPERTS) ** (-0.5)
    zero_low = jnp.zeros((), jnp.bfloat16)
    expert_iota = lax.iota(jnp.int32, n_window)
    named_hits = expert_ids[:, :, None] == expert_iota[None, None, :]
    picked = jnp.sum(named_hits.astype(jnp.int32), axis=1)
    weight_of = jnp.sum(jnp.where(named_hits, gate_weights[:, :, None], 0.0), axis=1)
    before = jnp.cumsum(picked, axis=0) - picked
    slot_iota = lax.iota(jnp.int32, capacity)
    placed = (before[None, :, :] == slot_iota[:, None, None]) & (picked[None, :, :] > 0)
    row_iota = lax.iota(jnp.int32, tok_count)
    slot_row = jnp.sum(jnp.where(placed, row_iota[None, :, None], 0), axis=1)
    slot_live = jnp.any(placed, axis=1)
    slot_gate = jnp.sum(jnp.where(placed, weight_of[None, :, :], 0.0), axis=1)
    slot_tokens = jnp.where(slot_live[:, :, None], tokens[slot_row], zero_low)
    slot_cotan = jnp.where(slot_live[:, :, None], cotangent[slot_row], zero_low)
    slot_dout = (slot_cotan.astype(jnp.float32) * slot_gate[:, :, None]).astype(jnp.bfloat16)
    rows_mine, dout_mine = (
        lax.all_to_all(slot_tokens, "sub", split_axis=1, concat_axis=0, tiled=True),
        lax.all_to_all(slot_dout, "sub", split_axis=1, concat_axis=0, tiled=True),
    )
    rows_all, dout_all = (
        lax.all_gather(rows_mine, "rep", axis=0, tiled=True),
        lax.all_gather(dout_mine, "rep", axis=0, tiled=True),
    )
    full_gate, full_up, full_down = (
        lax.all_gather(w_gate, "blk", axis=2, tiled=True),
        lax.all_gather(w_up, "blk", axis=2, tiled=True),
        lax.all_gather(w_down, "blk", axis=2, tiled=True),
    )
    pre_gate = jnp.einsum("red,efd->ref", rows_all, full_gate, preferred_element_type=jnp.float32)
    pre_up = jnp.einsum("red,efd->ref", rows_all, full_up, preferred_element_type=jnp.float32)
    activated, silu_slope = silu_pair(pre_gate)
    hidden = (activated * pre_up).astype(jnp.bfloat16)
    out_sum = lax.psum_scatter(
        jnp.einsum("ref,efd->red", hidden, full_down, preferred_element_type=jnp.float32).astype(
            jnp.bfloat16
        ),
        "rep",
        scatter_dimension=0,
        tiled=True,
    )
    slot_out = lax.all_to_all(out_sum, "sub", split_axis=0, concat_axis=1, tiled=True)
    down_term = (
        jnp.einsum("ref,red->efd", hidden, dout_all, preferred_element_type=jnp.float32)
        * grad_scale
    ).astype(jnp.bfloat16)
    down_back = lax.all_to_all(down_term[None], "blk", split_axis=3, concat_axis=0, tiled=True)
    down_owned = jnp.sum(down_back.astype(jnp.float32), axis=0)
    placed_low = placed.astype(jnp.bfloat16)
    mixed_acc = jnp.zeros((tok_count, tokens.shape[1]), jnp.float32)
    for expert in range(n_window):
        picked_rows = jnp.einsum(
            "ct,cd->td",
            placed_low[:, :, expert],
            slot_out[:, expert],
            preferred_element_type=jnp.float32,
        )
        mixed_acc = mixed_acc + weight_of[:, expert : expert + 1] * picked_rows
    mixed = mixed_acc.astype(jnp.bfloat16)
    slot_dot = jnp.sum(slot_cotan.astype(jnp.float32) * slot_out.astype(jnp.float32), axis=2)
    token_dot = jnp.sum(jnp.where(placed, slot_dot[:, None, :], 0.0), axis=0)
    gate_grad = jnp.sum(jnp.where(named_hits, token_dot[:, None, :], 0.0), axis=2)
    dhidden = jnp.einsum("red,efd->ref", dout_all, full_down, preferred_element_type=jnp.float32)
    dpre_gate = (dhidden * pre_up * silu_slope).astype(jnp.bfloat16)
    dpre_up = (dhidden * activated).astype(jnp.bfloat16)
    first = jnp.einsum("ref,efd->red", dpre_gate, full_gate, preferred_element_type=jnp.float32)
    in_sum = lax.psum_scatter(
        (
            first + jnp.einsum("ref,efd->red", dpre_up, full_up, preferred_element_type=jnp.float32)
        ).astype(jnp.bfloat16),
        "rep",
        scatter_dimension=0,
        tiled=True,
    )
    slot_in = lax.all_to_all(in_sum, "sub", split_axis=0, concat_axis=1, tiled=True)
    token_grad = jnp.einsum(
        "cte,ced->td", placed_low, slot_in, preferred_element_type=jnp.float32
    ).astype(jnp.bfloat16)
    both_pre = jnp.stack([dpre_gate, dpre_up])
    proj_term = (
        jnp.einsum("gref,red->gefd", both_pre, rows_all, preferred_element_type=jnp.float32)
        * grad_scale
    ).astype(jnp.bfloat16)
    proj_back = lax.all_to_all(proj_term[None], "blk", split_axis=4, concat_axis=0, tiled=True)
    proj_owned = jnp.sum(proj_back.astype(jnp.float32), axis=0)
    grad_gate = proj_owned[0]
    grad_up = proj_owned[1]
    return (mixed, token_grad, gate_grad, grad_gate, grad_up, down_owned)


def solution(mesh):
    in_specs = (
        P(("dom", "blk", "sub", "rep"), None),
        P(("dom", "blk", "sub", "rep"), None),
        P(("dom", "blk", "sub", "rep"), None),
        P("sub", "rep", "blk"),
        P("sub", "rep", "blk"),
        P("sub", "rep", "blk"),
        P(("dom", "blk", "sub", "rep"), None),
    )
    out_specs = (
        P(("dom", "blk", "sub", "rep"), None),
        P(("dom", "blk", "sub", "rep"), None),
        P(("dom", "blk", "sub", "rep"), None),
        P(("dom", "sub"), "rep", "blk"),
        P(("dom", "sub"), "rep", "blk"),
        P(("dom", "sub"), "rep", "blk"),
    )
    return jax.shard_map(
        on_device, mesh=mesh, in_specs=in_specs, out_specs=out_specs, check_vma=False
    )
```

profile of v0, /device:TPU:0, one launch (start us, length us, event | category | flops | bytes accessed | tf_op | source)
XLA Modules:
  0.0 349.1 jit_solution(12591786999858448248)
XLA Ops:
  7.2 0.7 all-gather.6.cloned.1.call-update
  8.0 0.7 all-gather.4.cloned.1.call-update
  8.7 0.7 all-gather.8.cloned.1.call-update
  9.4 0.7 convert_reduce_fusion.1
  10.9 0.6 gather_fusion
  11.8 8.5 %all_to_all.90 = bf16[12,2,2048]{2,0,1:T(8,128)(2,1)S(1)} all-to-all(bf16[12,2,2048]{2,0,1:T(8,128)(2,1)S(1)} %copy_select_fusion.1), channel_id=1, replica_groups=mesh['dom'=2,'blk'=4,'sub'=2,'rep'=2] {'sub'}, dimensions={1} | all-to-all | bytes 196608 | tf_op jit(solution)/shard_map/all_to_all | solution.py:39
  20.3 1.9 all_gather.15
  22.3 27.1 %all-gather.6.cloned.1.call-done = bf16[1,384,2048]{2,1,0:T(8,128)(2,1)} async-done(((bf16[1,384,512]{2,1,0:T(8,128)(2,1)}), bf16[1,384,2048]{2,1,0:T(8,128)(2,1)}) %all-gather.6.cloned.1.call-update) | async-done | bytes 1572880 | tf_op jit(solution)/shard_map/all_gather | solution.py:48
  49.3 2.0 fusion.21
  51.3 35.5 %all-gather.4.cloned.1.call-done = bf16[1,384,2048]{2,1,0:T(8,128)(2,1)} async-done(((bf16[1,384,512]{2,1,0:T(8,128)(2,1)}), bf16[1,384,2048]{2,1,0:T(8,128)(2,1)}) %all-gather.4.cloned.1.call-update) | async-done | bytes 1572880 | tf_op jit(solution)/shard_map/all_gather | solution.py:47
  86.8 2.0 fusion.18
  88.9 35.5 %all-gather.8.cloned.1.call-done = bf16[1,384,2048]{2,1,0:T(8,128)(2,1)} async-done(((bf16[1,384,512]{2,1,0:T(8,128)(2,1)}), bf16[1,384,2048]{2,1,0:T(8,128)(2,1)}) %all-gather.8.cloned.1.call-update) | async-done | bytes 1572880 | tf_op jit(solution)/shard_map/all_gather | solution.py:49
  124.3 2.5 fusion.6
  126.8 6.7 %reduce-scatter.3.cloned.1.call-done = bf16[24,1,2048]{2,0,1:T(8,128)(2,1)} async-done(((bf16[48,1,2048]{2,0,1:T(8,128)(2,1)}), bf16[24,1,2048]{2,0,1:T(8,128)(2,1)}) %reduce-scatter.3.cloned.1.call-update) | async-done | bytes 98320 | tf_op jit(solution)/shard_map/reduce_scatter | solution.py:55
  134.0 1.6 reduce.10
  135.6 0.8 reshape.167
  136.4 3.3 all-to-all-start.1
  139.8 0.6 gather_fusion.1
  140.5 3.5 %all-to-all-done.1 = bf16[2,2,12288]{2,1,0:T(2,128)(2,1)S(1)} async-done(((bf16[2,2,12288]{2,1,0:T(2,128)(2,1)}), bf16[2,2,12288]{2,1,0:T(2,128)(2,1)S(1)}, u32[]{:S(2)}, u32[]{:S(2)}) %all-to-all-start.1) | async-done | bytes 98336 | tf_op jit(solution)/shard_map/all_to_all | solution.py:63
  145.0 0.6 select_reduce_fusion.3
  145.8 6.8 %all_to_all.91 = bf16[12,2,2048]{2,0,1:T(8,128)(2,1)S(1)} all-to-all(bf16[12,2,2048]{2,0,1:T(8,128)(2,1)S(1)} %fusion.27), channel_id=1, replica_groups=mesh['dom'=2,'blk'=4,'sub'=2,'rep'=2] {'sub'}, dimensions={1} | all-to-all | bytes 196608 | tf_op jit(solution)/shard_map/all_to_all | solution.py:40
  152.6 1.9 all_gather.19
  154.6 2.1 multiply_convert_fusion.2
  157.1 1.1 fusion.7
  158.2 8.0 %reduce-scatter.5.cloned.1.call-done = bf16[24,1,2048]{2,0,1:T(8,128)(2,1)} async-done(((bf16[48,1,2048]{2,0,1:T(8,128)(2,1)}), bf16[24,1,2048]{2,0,1:T(8,128)(2,1)}) %reduce-scatter.5.cloned.1.call-update) | async-done | bytes 98320 | tf_op jit(solution)/shard_map/reduce_scatter | solution.py:88
  166.2 1.6 reduce.11
  167.8 0.8 reshape.171
  168.6 3.3 all-to-all-start.3
  171.9 0.6 fusion.1
  172.5 5.6 %copy.68 = bf16[1,1,384,2048]{2,1,0,3:T(2,128)(2,1)} copy(bf16[1,1,384,2048]{3,2,1,0:T(8,128)(2,1)S(1)} %fusion.1) | data formatting | bytes 3145728 | tf_op jit(solution)/shard_map/broadcast_in_dim | solution.py:68
  178.1 34.3 %reduce.12 = bf16[2048,384]{1,0:T(8,128)(2,1)S(1)} reduce(bf16[2048,1,1,384]{3,2,1,0:T(2,128)(2,1)} %bitcast.140, bf16[]{:T(256)} %broadcast.59), dimensions={1,2}, to_apply=%bitcast.132.reduce_sub_computation | reduce | bytes 3145730
  212.4 1.9 reshape.169
  214.3 4.8 %all-to-all-start.5 = ((bf16[4,2,98304]{2,1,0:T(2,128)(2,1)}), bf16[4,2,98304]{2,1,0:T(2,128)(2,1)S(1)}, u32[]{:S(2)}, u32[]{:S(2)}) async-start(bf16[4,2,98304]{2,1,0:T(2,128)(2,1)} %reshape.169), calls=%async_computation.7 | async-start | bytes 3145728 | tf_op jit(solution)/shard_map/all_to_all | solution.py:68
  219.1 1.0 fusion
  220.1 28.4 %copy.66 = bf16[1,2,1,384,2048]{3,1,2,0,4:T(2,128)(2,1)} copy(bf16[1,2,1,384,2048]{3,4,1,2,0:T(8,128)(2,1)S(1)} %fusion) | data formatting | bytes 6291456 | tf_op jit(solution)/shard_map/broadcast_in_dim | solution.py:105
  248.6 8.0 %all-to-all-done.5 = bf16[4,2,98304]{2,1,0:T(2,128)(2,1)S(1)} async-done(((bf16[4,2,98304]{2,1,0:T(2,128)(2,1)}), bf16[4,2,98304]{2,1,0:T(2,128)(2,1)S(1)}, u32[]{:S(2)}, u32[]{:S(2)}) %all-to-all-start.5) | async-done | bytes 1572896 | tf_op jit(solution)/shard_map/all_to_all | solution.py:68
  256.6 4.9 %all-to-all-start.4 = ((bf16[1,2,1,384,2048]{3,1,2,0,4:T(2,128)(2,1)}), bf16[1,2,1,384,2048]{3,1,2,0,4:T(2,128)(2,1)}, u32[]{:S(2)}, u32[]{:S(2)}) async-start(bf16[1,2,1,384,2048]{3,1,2,0,4:T(2,128)(2,1)} %copy.66), calls=%async_computation.6 | async-start | bytes 6291456 | tf_op jit(solution)/shard_map/all_to_all | solution.py:105
  261.8 1.1 fusion.3
  263.7 1.1 fusion.4
  264.8 2.9 reshape.170
  267.7 3.7 %copy.74 = f32[1,1,384,2048]{2,3,0,1:T(8,128)} copy(bf16[1,1,384,2048]{2,1,0,3:T(2,128)(2,1)} %bitcast.142) | data formatting | bytes 4718592
  271.4 2.1 reduce_sum.94
  273.5 1.1 copy.71
  274.7 56.9 %all-to-all-done.4 = bf16[1,2,1,384,2048]{3,1,2,0,4:T(2,128)(2,1)} async-done(((bf16[1,2,1,384,2048]{3,1,2,0,4:T(2,128)(2,1)}), bf16[1,2,1,384,2048]{3,1,2,0,4:T(2,128)(2,1)}, u32[]{:S(2)}, u32[]{:S(2)}) %all-to-all-start.4) | async-done | bytes 3145760 | tf_op jit(solution)/shard_map/all_to_all | solution.py:105
  331.6 5.7 %convert_reduce_fusion = f32[2,384,512]{1,0,2:T(2,128)S(1)} fusion(bf16[2,384,4,512]{1,0,3,2:T(2,128)(2,1)} %bitcast.65), kind=kLoop, calls=%fused_computation.2 | loop fusion | flops 2752512 | bytes 4718592 | tf_op jit(solution)/shard_map/reduce_sum | solution.py:106
  337.3 1.2 fusion.45
  338.5 2.1 copy.70
  340.6 2.0 copy.69
  (51 shorter events, 4.5 us)
Async XLA Ops:
  7.2 3.7 %copy-start = (bf16[128,2048]{1,0:T(8,128)(2,1)S(1)}, bf16[128,2048]{1,0:T(8,128)(2,1)}, u32[]{:S(2)}) copy-start(bf16[128,2048]{1,0:T(8,128)(2,1)} %param.7) | copy-start | bytes 1572868
  7.2 42.2 %all-gather.6.cloned.1.call-start = ((), (), s32[]{:S(2)}) async-start(), calls=%async_computation.9 | async-start | bytes 1966080 | tf_op jit(solution)/shard_map/all_gather | solution.py:48
  7.9 78.9 %all-gather.4.cloned.1.call-start = ((), (), s32[]{:S(2)}) async-start(), calls=%async_computation.8 | async-start | bytes 1966080 | tf_op jit(solution)/shard_map/all_gather | solution.py:47
  8.7 115.7 %all-gather.8.cloned.1.call-start = ((), (), s32[]{:S(2)}) async-start(), calls=%async_computation.10 | async-start | bytes 1966080 | tf_op jit(solution)/shard_map/all_gather | solution.py:49
  9.4 124.1 %reduce-scatter.3.cloned.1.call-start = ((), (), s32[]{:S(2)}) async-start(), calls=%async_computation.11 | async-start | bytes 294912 | tf_op jit(solution)/shard_map/reduce_scatter | solution.py:55
  88.8 50.9 %copy-start.3 = (bf16[128,2048]{1,0:T(8,128)(2,1)S(1)}, bf16[128,2048]{1,0:T(8,128)(2,1)}, u32[]{:S(2)}) copy-start(bf16[128,2048]{1,0:T(8,128)(2,1)} %param.13) | copy-start | bytes 1572868
  126.8 18.2 %copy-start.4 = (s32[128,8]{0,1:T(8,128)S(1)}, s32[128,8]{0,1:T(8,128)}, u32[]{:S(2)}) copy-start(s32[128,8]{0,1:T(8,128)} %param.8) | copy-start | bytes 12292
  126.8 18.2 %copy-start.5 = (f32[128,8]{0,1:T(8,128)S(1)}, f32[128,8]{0,1:T(8,128)}, u32[]{:S(2)}) copy-start(f32[128,8]{0,1:T(8,128)} %param.9) | copy-start | bytes 12292
  136.4 7.6 %all-to-all-start.1 = ((bf16[2,2,12288]{2,1,0:T(2,128)(2,1)}), bf16[2,2,12288]{2,1,0:T(2,128)(2,1)S(1)}, u32[]{:S(2)}, u32[]{:S(2)}) async-start(bf16[2,2,12288]{2,1,0:T(2,128)(2,1)} %reshape.167), calls=%async_computation.2 | async-start | bytes 196608 | tf_op jit(solution)/shard_map/all_to_all | solution.py:63
  139.7 26.5 %reduce-scatter.5.cloned.1.call-start = ((), (), s32[]{:S(2)}) async-start(), calls=%async_computation.12 | async-start | bytes 294912 | tf_op jit(solution)/shard_map/reduce_scatter | solution.py:88
  144.8 11.9 %copy-start.2 = (bf16[1,384,2048]{2,1,0:T(8,128)(2,1)S(1)}, bf16[1,384,2048]{2,1,0:T(8,128)(2,1)}, u32[]{:S(2)}) copy-start(bf16[1,384,2048]{2,1,0:T(8,128)(2,1)} %all-gather.4.cloned.1.call-done) | copy-start | bytes 4718596
  154.6 2.5 copy-start.1
  168.6 45.7 %all-to-all-start.3 = ((bf16[2,2,12288]{2,1,0:T(2,128)(2,1)}), bf16[2,2,12288]{2,1,0:T(2,128)(2,1)S(1)}, u32[]{:S(2)}, u32[]{:S(2)}) async-start(bf16[2,2,12288]{2,1,0:T(2,128)(2,1)} %reshape.171), calls=%async_computation.5 | async-start | bytes 196608 | tf_op jit(solution)/shard_map/all_to_all | solution.py:96
  214.3 42.3 %all-to-all-start.5 = ((bf16[4,2,98304]{2,1,0:T(2,128)(2,1)}), bf16[4,2,98304]{2,1,0:T(2,128)(2,1)S(1)}, u32[]{:S(2)}, u32[]{:S(2)}) async-start(bf16[4,2,98304]{2,1,0:T(2,128)(2,1)} %reshape.169), calls=%async_computation.7 | async-start | bytes 3145728 | tf_op jit(solution)/shard_map/all_to_all | solution.py:68
  256.6 75.0 %all-to-all-start.4 = ((bf16[1,2,1,384,2048]{3,1,2,0,4:T(2,128)(2,1)}), bf16[1,2,1,384,2048]{3,1,2,0,4:T(2,128)(2,1)}, u32[]{:S(2)}, u32[]{:S(2)}) async-start(bf16[1,2,1,384,2048]{3,1,2,0,4:T(2,128)(2,1)} %copy.66), calls=%async_computation.6 | async-start | bytes 6291456 | tf_op jit(solution)/shard_map/all_to_all | solution.py:105
Sparse Core Ops, SparseCore 0:
  9.6 39.7 all-gather.5
  50.9 35.8 all-gather.3
  88.4 35.8 all-gather.7
  127.0 6.4 reduce-scatter.2
  158.3 7.8 reduce-scatter.4
where the time goes:
time: 350 us; the launch traced here: 349 us
  waiting for transfers between devices  183 us (52%)
  local copies, waits for them, and re-layouts  53.1 us (15%)
  other arithmetic  48.7 us (14%)
  blocking collectives  19.3 us (6%)
  starting transfers between devices  16.5 us (5%)
  matrix products  14.2 us (4%)
  between operations  14.1 us (4%)
    all_to_all x1, waiting for transfers between devices, on_device(): lax.all_to_all(proj_term[None], 'blk', split_axis=4, concat_axis=0, tiled...  56.9 us
    all_gather x1, waiting for transfers between devices, on_device(): lax.all_gather(w_gate, 'blk', axis=2, tiled=True)  35.5 us
    all_gather x1, waiting for transfers between devices, on_device(): lax.all_gather(w_down, 'blk', axis=2, tiled=True)  35.5 us
    unnamed x1, other arithmetic  34.3 us
    broadcast_in_dim x1, local copies, waits for them, and re-layouts, on_device(): proj_term[None]  28.4 us
    all_gather x1, waiting for transfers between devices, on_device(): lax.all_gather(w_up, 'blk', axis=2, tiled=True)  27.1 us
    unnamed x22, local copies, waits for them, and re-layouts  15.4 us
    all_to_all x1, blocking collectives, on_device(): lax.all_to_all(slot_tokens, 'sub', split_axis=1, concat_axis=0, tiled=True)  8.51 us
  transfers between devices with their start and end apart: 9, of which 8 were waited for; matrix products, arithmetic and copies ran while one was open for 26% of the time, Pallas kernels for 0%

commit v1 on v0

--- a/solution.py
+++ b/solution.py
@@ -6,6 +6,28 @@
 NUM_EXPERTS = 128
 TOPK = 8
 CAP = 12
+
+
+def laid_out(tiles, dim):
+    tiles = jnp.moveaxis(tiles, 0, dim)
+    shape = tiles.shape
+    return tiles.reshape(*shape[:dim], shape[dim] * shape[dim + 1], *shape[dim + 2 :])
+
+
+def gather_around(x, axis, dim):
+    size = lax.axis_size(axis)
+    pairs = [(i, (i + 1) % size) for i in range(size)]
+    back = [(b, a) for a, b in pairs]
+    lower, upper = ([], [])
+    for step in range(size - 1):
+        if step % 2 == 0:
+            lower.append(lax.ppermute(lower[-1] if lower else x, axis, pairs))
+        else:
+            upper.append(lax.ppermute(upper[-1] if upper else x, axis, back))
+    parts = jnp.stack([*lower[::-1], x, *upper])
+    shift = lax.axis_index(axis) - len(lower)
+    parts = parts[(jnp.arange(size) - shift) % size]
+    return laid_out(parts, dim)
 
 
 def silu_pair(pre_act):
@@ -45,7 +67,7 @@
     )
     full_gate, full_up, full_down = (
         lax.all_gather(w_gate, "blk", axis=2, tiled=True),
-        lax.all_gather(w_up, "blk", axis=2, tiled=True),
+        gather_around(w_up, "blk", 2),
         lax.all_gather(w_down, "blk", axis=2, tiled=True),
     )
     pre_gate = jnp.einsum("red,efd->ref", rows_all, full_gate, preferred_element_type=jnp.float32)

time: 350 us -> 329 us (0.940)
  waiting for transfers between devices: 183 us -> 157 us
  starting transfers between devices: 16.5 us -> 25.3 us
  blocking collectives: 19.3 us -> 10.9 us
  local copies, waits for them, and re-layouts: 53.1 us -> 57.5 us
    all_gather x1, waiting for transfers between devices: 35.5 us -> 3.94 us  [on_device(): lax.all_gather(w_gate, 'blk', axis=2, tiled=True)]
    ppermute x0 -> x3, waiting for transfers between devices: none -> 28.7 us  [the longest x1 19.5 us: gather_around(): upper.append(lax.ppermute(upper[-1] if upper else x, axis, back))]
    all_gather x1 -> x0, waiting for transfers between devices: 27.1 us -> none  [on_device(): lax.all_gather(w_up, 'blk', axis=2, tiled=True)]
    all_to_all x1 -> x0, blocking collectives: 8.51 us -> none  [on_device(): lax.all_to_all(slot_tokens, 'sub', split_axis=1, concat_axis=0, tiled=True)]
    ppermute x0 -> x3, starting transfers between devices: none -> 5.47 us  [the longest x2 3.38 us: gather_around(): lower.append(lax.ppermute(lower[-1] if lower else x, axis, pairs))]
    all_to_all x0 -> x1, waiting for transfers between devices: none -> 4.37 us  [on_device(): lax.all_to_all(slot_tokens, 'sub', split_axis=1, concat_axis=0, tiled=True)]
    unnamed x22 -> x24, local copies, waits for them, and re-layouts: 15.4 us -> 16.2 us
  transfers between devices with their start and end apart: 9 -> 12, of which waited for: 8 -> 11; matrix products, arithmetic and copies ran while one was open for 26% -> 29% of each run, Pallas kernels for 0% -> 0%
where the time goes in v1:
time: 329 us; the launch traced here: 328 us
  waiting for transfers between devices  157 us (48%)
  local copies, waits for them, and re-layouts  57.5 us (17%)
  other arithmetic  50.5 us (15%)
  starting transfers between devices  25.3 us (8%)
  between operations  14.1 us (4%)
  matrix products  12.7 us (4%)
  blocking collectives  10.9 us (3%)
    all_to_all x1, waiting for transfers between devices, on_device(): lax.all_to_all(proj_term[None], 'blk', split_axis=4, concat_axis=0, tiled...  57.2 us
    all_gather x1, waiting for transfers between devices, on_device(): lax.all_gather(w_down, 'blk', axis=2, tiled=True)  35.9 us
    unnamed x1, other arithmetic  34.3 us
    broadcast_in_dim x1, local copies, waits for them, and re-layouts, on_device(): proj_term[None]  28.4 us
    ppermute x1, waiting for transfers between devices, gather_around(): upper.append(lax.ppermute(upper[-1] if upper else x, axis, back))  19.5 us
    unnamed x24, local copies, waits for them, and re-layouts  16.2 us
    ppermute x2, waiting for transfers between devices, gather_around(): lower.append(lax.ppermute(lower[-1] if lower else x, axis, pairs))  9.22 us
    all_to_all x1, waiting for transfers between devices, on_device(): lax.all_to_all(down_term[None], 'blk', split_axis=3, concat_axis=0, tiled...  8.04 us
  transfers between devices with their start and end apart: 12, of which 11 were waited for; matrix products, arithmetic and copies ran while one was open for 29% of the time, Pallas kernels for 0%

profile of v1, /device:TPU:0, one launch (start us, length us, event | category | flops | bytes accessed | tf_op | source)
XLA Modules:
  0.0 328.3 jit_solution(10544516583501412706)
XLA Ops:
  8.0 3.1 collective-permute-start
  11.1 2.1 collective-permute-start.2
  15.4 7.9 %collective-permute-done = bf16[1,384,512]{2,1,0:T(8,128)(2,1)S(1)} collective-permute-done((bf16[1,384,512]{2,1,0:T(8,128)(2,1)}, bf16[1,384,512]{2,1,0:T(8,128)(2,1)S(1)}, u32[]{:S(2)}, u32[]{:S(2)}) %collective-permute-start) | collective-permute-done | bytes 393248 | tf_op jit(solution)/shard_map/ppermute | solution.py:24
  24.3 3.4 %all-to-all-start = ((bf16[12,2,2048]{2,0,1:T(8,128)(2,1)}), bf16[12,2,2048]{2,0,1:T(8,128)(2,1)S(1)}, u32[]{:S(2)}, u32[]{:S(2)}) async-start(bf16[12,2,2048]{2,0,1:T(8,128)(2,1)} %copy_select_fusion.1), calls=%async_computation | async-start | bytes 262144 | tf_op jit(solution)/shard_map/all_to_all | solution.py:61
  27.8 4.4 %all-to-all-done = bf16[12,2,2048]{2,0,1:T(8,128)(2,1)S(1)} async-done(((bf16[12,2,2048]{2,0,1:T(8,128)(2,1)}), bf16[12,2,2048]{2,0,1:T(8,128)(2,1)S(1)}, u32[]{:S(2)}, u32[]{:S(2)}) %all-to-all-start) | async-done | bytes 98336 | tf_op jit(solution)/shard_map/all_to_all | solution.py:61
  32.2 1.9 all_gather.12
  34.2 19.5 %collective-permute-done.2 = bf16[1,384,512]{2,1,0:T(8,128)(2,1)S(1)} collective-permute-done((bf16[1,384,512]{2,1,0:T(8,128)(2,1)}, bf16[1,384,512]{2,1,0:T(8,128)(2,1)S(1)}, u32[]{:S(2)}, u32[]{:S(2)}) %collective-permute-start.2) | collective-permute-done | bytes 393248 | tf_op jit(solution)/shard_map/ppermute | solution.py:26
  53.6 1.3 collective-permute-done.1
  55.0 0.7 copy-done.4
  55.7 1.2 maximum_bitcast_fusion
  56.9 1.8 gather_fusion.1
  58.7 1.9 copy.77
  61.0 3.9 %all-gather.3.cloned.1.call-done = bf16[1,384,2048]{2,1,0:T(8,128)(2,1)} async-done(((bf16[1,384,512]{2,1,0:T(8,128)(2,1)}), bf16[1,384,2048]{2,1,0:T(8,128)(2,1)}) %all-gather.3.cloned.1.call-update) | async-done | bytes 1572880 | tf_op jit(solution)/shard_map/all_gather | solution.py:69
  64.9 2.0 fusion.14
  67.0 35.9 %all-gather.5.cloned.1.call-done = bf16[1,384,2048]{2,1,0:T(8,128)(2,1)} async-done(((bf16[1,384,512]{2,1,0:T(8,128)(2,1)}), bf16[1,384,2048]{2,1,0:T(8,128)(2,1)}) %all-gather.5.cloned.1.call-update) | async-done | bytes 1572880 | tf_op jit(solution)/shard_map/all_gather | solution.py:71
  102.9 2.5 fusion.6
  105.4 6.8 %reduce-scatter.3.cloned.1.call-done = bf16[24,1,2048]{2,0,1:T(8,128)(2,1)} async-done(((bf16[48,1,2048]{2,0,1:T(8,128)(2,1)}), bf16[24,1,2048]{2,0,1:T(8,128)(2,1)}) %reduce-scatter.3.cloned.1.call-update) | async-done | bytes 98320 | tf_op jit(solution)/shard_map/reduce_scatter | solution.py:77
  112.8 1.6 reduce.10
  114.3 0.8 reshape.231
  115.1 3.3 %all-to-all-start.1 = ((bf16[2,2,12288]{2,1,0:T(2,128)(2,1)}), bf16[2,2,12288]{2,1,0:T(2,128)(2,1)S(1)}, u32[]{:S(2)}, u32[]{:S(2)}) async-start(bf16[2,2,12288]{2,1,0:T(2,128)(2,1)} %reshape.231), calls=%async_computation.2 | async-start | bytes 196608 | tf_op jit(solution)/shard_map/all_to_all | solution.py:85
  119.2 3.5 %all-to-all-done.1 = bf16[2,2,12288]{2,1,0:T(2,128)(2,1)S(1)} async-done(((bf16[2,2,12288]{2,1,0:T(2,128)(2,1)}), bf16[2,2,12288]{2,1,0:T(2,128)(2,1)S(1)}, u32[]{:S(2)}, u32[]{:S(2)}) %all-to-all-start.1) | async-done | bytes 98336 | tf_op jit(solution)/shard_map/all_to_all | solution.py:85
  124.5 6.8 %all_to_all.90 = bf16[12,2,2048]{2,0,1:T(8,128)(2,1)S(1)} all-to-all(bf16[12,2,2048]{2,0,1:T(8,128)(2,1)S(1)} %fusion.20), channel_id=1, replica_groups=mesh['dom'=2,'blk'=4,'sub'=2,'rep'=2] {'sub'}, dimensions={1} | all-to-all | bytes 196608 | tf_op jit(solution)/shard_map/all_to_all | solution.py:62
  131.4 2.1 all_gather.15
  133.5 2.0 multiply_convert_fusion.2
  135.9 1.3 fusion.7
  137.2 8.0 %reduce-scatter.5.cloned.1.call-done = bf16[24,1,2048]{2,0,1:T(8,128)(2,1)} async-done(((bf16[48,1,2048]{2,0,1:T(8,128)(2,1)}), bf16[24,1,2048]{2,0,1:T(8,128)(2,1)}) %reduce-scatter.5.cloned.1.call-update) | async-done | bytes 98320 | tf_op jit(solution)/shard_map/reduce_scatter | solution.py:110
  145.2 1.6 reduce.11
  146.8 0.8 reshape.235
  147.5 3.3 %all-to-all-start.3 = ((bf16[2,2,12288]{2,1,0:T(2,128)(2,1)}), bf16[2,2,12288]{2,1,0:T(2,128)(2,1)S(1)}, u32[]{:S(2)}, u32[]{:S(2)}) async-start(bf16[2,2,12288]{2,1,0:T(2,128)(2,1)} %reshape.235), calls=%async_computation.5 | async-start | bytes 196608 | tf_op jit(solution)/shard_map/all_to_all | solution.py:118
  151.4 5.6 %copy.83 = bf16[1,1,384,2048]{2,1,0,3:T(2,128)(2,1)} copy(bf16[1,1,384,2048]{3,2,1,0:T(8,128)(2,1)S(1)} %fusion.1) | data formatting | bytes 3145728 | tf_op jit(solution)/shard_map/broadcast_in_dim | solution.py:90
  157.1 34.3 %reduce.12 = bf16[2048,384]{1,0:T(8,128)(2,1)S(1)} reduce(bf16[2048,1,1,384]{3,2,1,0:T(2,128)(2,1)} %bitcast.149, bf16[]{:T(256)} %broadcast.128), dimensions={1,2}, to_apply=%bitcast.137.reduce_sub_computation | reduce | bytes 3145730
  191.4 1.9 reshape.233
  193.3 5.0 %all-to-all-start.5 = ((bf16[4,2,98304]{2,1,0:T(2,128)(2,1)}), bf16[4,2,98304]{2,1,0:T(2,128)(2,1)S(1)}, u32[]{:S(2)}, u32[]{:S(2)}) async-start(bf16[4,2,98304]{2,1,0:T(2,128)(2,1)} %reshape.233), calls=%async_computation.7 | async-start | bytes 3145728 | tf_op jit(solution)/shard_map/all_to_all | solution.py:90
  198.3 1.0 fusion
  199.3 28.4 %copy.81 = bf16[1,2,1,384,2048]{3,1,2,0,4:T(2,128)(2,1)} copy(bf16[1,2,1,384,2048]{3,4,1,2,0:T(8,128)(2,1)S(1)} %fusion) | data formatting | bytes 6291456 | tf_op jit(solution)/shard_map/broadcast_in_dim | solution.py:127
  227.7 8.0 %all-to-all-done.5 = bf16[4,2,98304]{2,1,0:T(2,128)(2,1)S(1)} async-done(((bf16[4,2,98304]{2,1,0:T(2,128)(2,1)}), bf16[4,2,98304]{2,1,0:T(2,128)(2,1)S(1)}, u32[]{:S(2)}, u32[]{:S(2)}) %all-to-all-start.5) | async-done | bytes 1572896 | tf_op jit(solution)/shard_map/all_to_all | solution.py:90
  235.7 4.6 %all-to-all-start.4 = ((bf16[1,2,1,384,2048]{3,1,2,0,4:T(2,128)(2,1)}), bf16[1,2,1,384,2048]{3,1,2,0,4:T(2,128)(2,1)}, u32[]{:S(2)}, u32[]{:S(2)}) async-start(bf16[1,2,1,384,2048]{3,1,2,0,4:T(2,128)(2,1)} %copy.81), calls=%async_computation.6 | async-start | bytes 6291456 | tf_op jit(solution)/shard_map/all_to_all | solution.py:127
  240.7 1.1 fusion.3
  242.6 1.1 fusion.4
  243.7 2.9 reshape.234
  246.6 3.7 %copy.89 = f32[1,1,384,2048]{2,3,0,1:T(8,128)} copy(bf16[1,1,384,2048]{2,1,0,3:T(2,128)(2,1)} %bitcast.151) | data formatting | bytes 4718592
  250.3 2.1 reduce_sum.94
  252.5 1.1 copy.86
  253.6 57.2 %all-to-all-done.4 = bf16[1,2,1,384,2048]{3,1,2,0,4:T(2,128)(2,1)} async-done(((bf16[1,2,1,384,2048]{3,1,2,0,4:T(2,128)(2,1)}), bf16[1,2,1,384,2048]{3,1,2,0,4:T(2,128)(2,1)}, u32[]{:S(2)}, u32[]{:S(2)}) %all-to-all-start.4) | async-done | bytes 3145760 | tf_op jit(solution)/shard_map/all_to_all | solution.py:127
  310.8 5.7 %convert_reduce_fusion = f32[2,384,512]{1,0,2:T(2,128)S(1)} fusion(bf16[2,384,4,512]{1,0,3,2:T(2,128)(2,1)} %bitcast.73), kind=kLoop, calls=%fused_computation.3 | loop fusion | flops 2752512 | bytes 4718592 | tf_op jit(solution)/shard_map/reduce_sum | solution.py:128
  316.4 1.2 fusion.40
  317.7 2.1 copy.85
  319.7 2.0 copy.84
  (62 shorter events, 9.6 us)
Async XLA Ops:
  7.2 7.4 %copy-start = (bf16[128,2048]{1,0:T(8,128)(2,1)S(1)}, bf16[128,2048]{1,0:T(8,128)(2,1)}, u32[]{:S(2)}) copy-start(bf16[128,2048]{1,0:T(8,128)(2,1)} %param.7) | copy-start | bytes 1572868
  7.2 57.7 %all-gather.3.cloned.1.call-start = ((), (), s32[]{:S(2)}) async-start(), calls=%async_computation.8 | async-start | bytes 1966080 | tf_op jit(solution)/shard_map/all_gather | solution.py:69
  7.9 47.8 %copy-start.3 = (bf16[1,384,512]{2,1,0:T(8,128)(2,1)S(1)}, bf16[1,384,512]{2,1,0:T(8,128)(2,1)}, u32[]{:S(2)}) copy-start(bf16[1,384,512]{2,1,0:T(8,128)(2,1)} %param.11) | copy-start | bytes 1179652
  7.9 95.0 %all-gather.5.cloned.1.call-start = ((), (), s32[]{:S(2)}) async-start(), calls=%async_computation.9 | async-start | bytes 1966080 | tf_op jit(solution)/shard_map/all_gather | solution.py:71
  8.0 15.3 %collective-permute-start = (bf16[1,384,512]{2,1,0:T(8,128)(2,1)}, bf16[1,384,512]{2,1,0:T(8,128)(2,1)S(1)}, u32[]{:S(2)}, u32[]{:S(2)}) collective-permute-start(bf16[1,384,512]{2,1,0:T(8,128)(2,1)} %param.11), channel_id=1, source_target_pairs={{0,4},{4,8},{8,12},{12,0},{1,5},{5,9},{9,13},{13,1},{2,6},{6,10},{... | collective-permute-start | bytes 1179656 | tf_op jit(solution)/shard_map/ppermute | solution.py:24
  11.1 42.6 %collective-permute-start.2 = (bf16[1,384,512]{2,1,0:T(8,128)(2,1)}, bf16[1,384,512]{2,1,0:T(8,128)(2,1)S(1)}, u32[]{:S(2)}, u32[]{:S(2)}) collective-permute-start(bf16[1,384,512]{2,1,0:T(8,128)(2,1)} %param.11), channel_id=1, source_target_pairs={{4,0},{8,4},{12,8},{0,12},{5,1},{9,5},{13,9},{1,13},{6,2},{10,6},{... | collective-permute-start | bytes 1179656 | tf_op jit(solution)/shard_map/ppermute | solution.py:26
  23.3 31.7 %collective-permute-start.1 = (bf16[1,384,512]{2,1,0:T(8,128)(2,1)S(1)}, bf16[1,384,512]{2,1,0:T(8,128)(2,1)S(1)}, u32[]{:S(2)}, u32[]{:S(2)}) collective-permute-start(bf16[1,384,512]{2,1,0:T(8,128)(2,1)S(1)} %collective-permute-done), channel_id=1, source_target_pairs={{0,4},{4,8},{8,12},{12,0},{1,5},{5,9},{9,13},{13,1},{2,6},{6,10},{... | collective-permute-start | bytes 1179656 | tf_op jit(solution)/shard_map/ppermute | solution.py:24
  24.3 7.8 %all-to-all-start = ((bf16[12,2,2048]{2,0,1:T(8,128)(2,1)}), bf16[12,2,2048]{2,0,1:T(8,128)(2,1)S(1)}, u32[]{:S(2)}, u32[]{:S(2)}) async-start(bf16[12,2,2048]{2,0,1:T(8,128)(2,1)} %copy_select_fusion.1), calls=%async_computation | async-start | bytes 262144 | tf_op jit(solution)/shard_map/all_to_all | solution.py:61
  27.7 84.5 %reduce-scatter.3.cloned.1.call-start = ((), (), s32[]{:S(2)}) async-start(), calls=%async_computation.10 | async-start | bytes 294912 | tf_op jit(solution)/shard_map/reduce_scatter | solution.py:77
  55.0 0.7 copy-start.4
  66.9 51.6 %copy-start.2 = (bf16[128,2048]{1,0:T(8,128)(2,1)S(1)}, bf16[128,2048]{1,0:T(8,128)(2,1)}, u32[]{:S(2)}) copy-start(bf16[128,2048]{1,0:T(8,128)(2,1)} %param.13) | copy-start | bytes 1572868
  105.4 18.3 %copy-start.5 = (s32[128,8]{0,1:T(8,128)S(1)}, s32[128,8]{0,1:T(8,128)}, u32[]{:S(2)}) copy-start(s32[128,8]{0,1:T(8,128)} %param.8) | copy-start | bytes 12292
  105.4 18.3 %copy-start.6 = (f32[128,8]{0,1:T(8,128)S(1)}, f32[128,8]{0,1:T(8,128)}, u32[]{:S(2)}) copy-start(f32[128,8]{0,1:T(8,128)} %param.9) | copy-start | bytes 12292
  115.1 7.6 %all-to-all-start.1 = ((bf16[2,2,12288]{2,1,0:T(2,128)(2,1)}), bf16[2,2,12288]{2,1,0:T(2,128)(2,1)S(1)}, u32[]{:S(2)}, u32[]{:S(2)}) async-start(bf16[2,2,12288]{2,1,0:T(2,128)(2,1)} %reshape.231), calls=%async_computation.2 | async-start | bytes 196608 | tf_op jit(solution)/shard_map/all_to_all | solution.py:85
  118.4 26.8 %reduce-scatter.5.cloned.1.call-start = ((), (), s32[]{:S(2)}) async-start(), calls=%async_computation.11 | async-start | bytes 294912 | tf_op jit(solution)/shard_map/reduce_scatter | solution.py:110
  131.4 4.1 %copy-start.1 = (bf16[1,384,2048]{2,1,0:T(8,128)(2,1)S(1)}, bf16[1,384,2048]{2,1,0:T(8,128)(2,1)}, u32[]{:S(2)}) copy-start(bf16[1,384,2048]{2,1,0:T(8,128)(2,1)} %all-gather.3.cloned.1.call-done) | copy-start | bytes 4718596
  147.5 45.7 %all-to-all-start.3 = ((bf16[2,2,12288]{2,1,0:T(2,128)(2,1)}), bf16[2,2,12288]{2,1,0:T(2,128)(2,1)S(1)}, u32[]{:S(2)}, u32[]{:S(2)}) async-start(bf16[2,2,12288]{2,1,0:T(2,128)(2,1)} %reshape.235), calls=%async_computation.5 | async-start | bytes 196608 | tf_op jit(solution)/shard_map/all_to_all | solution.py:118
  193.3 42.5 %all-to-all-start.5 = ((bf16[4,2,98304]{2,1,0:T(2,128)(2,1)}), bf16[4,2,98304]{2,1,0:T(2,128)(2,1)S(1)}, u32[]{:S(2)}, u32[]{:S(2)}) async-start(bf16[4,2,98304]{2,1,0:T(2,128)(2,1)} %reshape.233), calls=%async_computation.7 | async-start | bytes 3145728 | tf_op jit(solution)/shard_map/all_to_all | solution.py:90
  235.7 75.0 %all-to-all-start.4 = ((bf16[1,2,1,384,2048]{3,1,2,0,4:T(2,128)(2,1)}), bf16[1,2,1,384,2048]{3,1,2,0,4:T(2,128)(2,1)}, u32[]{:S(2)}, u32[]{:S(2)}) async-start(bf16[1,2,1,384,2048]{3,1,2,0,4:T(2,128)(2,1)} %copy.81), calls=%async_computation.6 | async-start | bytes 6291456 | tf_op jit(solution)/shard_map/all_to_all | solution.py:127
Sparse Core Ops, SparseCore 0:
  9.6 55.3 all-gather.2
  66.5 36.3 all-gather.4
  105.7 6.4 reduce-scatter.2
  137.3 7.8 reduce-scatter.4
